TPU v7x, 128 devices: a whole 4x4x4 slice. The times are simulated.
128 devices in a mesh: wide: 16 (over x, z_hi, core), narrow: 8 (over z_lo, y).
Axes of the slice: x: 4, y: 4, z: 4 (z_hi: 2, z_lo: 2; z = z_hi * 2 + z_lo), core: 2. Of those that a mesh axis runs over, the one named last changes fastest.
Arguments:
- activations: bfloat16 [2048, 16384], P('wide', 'narrow'), may hold values from -30 to 30, as said below
- weight_tile: bfloat16 [16384, 16384], P('wide', 'narrow'), may hold values from -3 to 3
- codes: int32 [16384, 16384], P('wide', 'narrow'), may hold values from -8 to 7
- group_scales: float32 [16384, 128], P('wide', 'narrow'), may hold values from 0.02 to 0.2
- right_factor: bfloat16 [16384, 256], replicated, may hold values from -0.046875 to 0.046875
Outputs:
- residual_product: float32 [16384, 256], P(('wide', 'narrow'))
- gram: float32 [256, 256], replicated
- hessian_tiles: bfloat16 [16384, 16384], P('wide', 'narrow')
Inputs may be any that keep to these rules, and one draw needn't show every extreme that they name: `activations`: each token's features are a product of a token scale, a feature scale and a value.
All inputs are finite; a program needn't handle non-finite values.
Results may differ from a plain program's by a relative error of at most 0.0049.
Values may be sent and summed in bfloat16 or wider, within the bound.
A program may use at most 128 MiB of HBM per device.

v0:
```python
import jax
import jax.numpy as jnp
from jax import lax
from jax.sharding import PartitionSpec as P


def body(activations, weight_tile, codes, group_scales, right_factor):
    rows_local = weight_tile.shape[0]
    cols_local = weight_tile.shape[1]
    wide_count = lax.axis_size("wide")
    narrow_count = lax.axis_size("narrow")
    wide_index = lax.axis_index("wide")
    narrow_index = lax.axis_index("narrow")
    total_tokens = activations.shape[0] * wide_count
    contract_first = (((0,), (0,)), ((), ()))
    full_features = lax.all_gather(activations, "narrow", axis=1, tiled=True)
    row_operand = lax.all_to_all(full_features, "wide", split_axis=1, concat_axis=0, tiled=True)
    hess_sum = lax.dot_general(
        row_operand,
        lax.all_gather(activations, "wide", axis=0, tiled=True),
        contract_first,
        preferred_element_type=jnp.float32,
    )
    hessian = hess_sum / total_tokens
    hessian_tiles = hessian.astype(jnp.bfloat16)
    groups = group_scales.shape[1]
    width = cols_local // groups
    quantized = (
        codes.reshape(rows_local, groups, width).astype(jnp.float32) * group_scales[:, :, None]
    ).reshape(rows_local, cols_local)
    residual = (weight_tile.astype(jnp.float32) - quantized).astype(jnp.bfloat16)
    right_cols = lax.dynamic_slice_in_dim(right_factor, narrow_index * cols_local, cols_local, 0)
    partial_value = jnp.dot(
        hessian, right_cols.astype(jnp.float32), precision=lax.Precision.HIGHEST
    )
    product_own = lax.psum(partial_value, "narrow").astype(jnp.bfloat16)
    product_full = lax.all_gather(product_own, "wide", axis=0, tiled=True)
    product_cols = lax.dynamic_slice_in_dim(product_full, narrow_index * cols_local, cols_local, 0)
    share = rows_local // narrow_count
    gram_start = wide_index * rows_local + narrow_index * share
    product_share = lax.dynamic_slice_in_dim(product_full, gram_start, share, 0)
    right_share = lax.dynamic_slice_in_dim(right_factor, gram_start, share, 0)
    gram_part = lax.dot_general(
        right_share, product_share, contract_first, preferred_element_type=jnp.float32
    )
    gram = lax.psum(gram_part, ("wide", "narrow"))
    residual_product = lax.psum_scatter(
        jnp.dot(residual, product_cols, preferred_element_type=jnp.float32),
        "narrow",
        scatter_dimension=0,
        tiled=True,
    )
    return (residual_product, gram, hessian_tiles)


def solution(mesh):
    in_specs = (
        P("wide", "narrow"),
        P("wide", "narrow"),
        P("wide", "narrow"),
        P("wide", "narrow"),
        P(),
    )
    out_specs = (P(("wide", "narrow"), None), P(), P("wide", "narrow"))
    return jax.shard_map(body, mesh=mesh, in_specs=in_specs, out_specs=out_specs, check_vma=False)
```

profile of v0, /device:TPU:0, one launch (start us, length us, event | category | flops | bytes accessed | tf_op | source)
XLA Modules:
  0.0 524.6 jit_solution(170166573466252105)
XLA Ops:
  7.2 0.0 all-gather.4.cloned.1.call-start
  7.2 2.0 copy.11
  9.3 0.0 all-gather.4.cloned.1.call-update
  9.3 0.0 all-gather.6.cloned.1.call-start
  9.3 0.7 all-gather.6.cloned.1.call-update
  10.0 55.3 %all-gather.4.cloned.1.call-done = bf16[128,16384]{0,1:T(8,128)(2,1)} async-done(((bf16[128,2048]{0,1:T(8,128)(2,1)}), bf16[128,16384]{0,1:T(8,128)(2,1)}) %all-gather.4.cloned.1.call-update) | async-done | bytes 4194320 | tf_op jit(solution)/shard_map/all_gather | solution.py:16
  65.3 6.7 %all-to-all-start = ((bf16[128,16,1024]{0,2,1:T(8,128)(2,1)}), bf16[128,16,1024]{0,2,1:T(8,128)(2,1)}, u32[]{:S(2)}, u32[]{:S(2)}) async-start(bf16[128,16,1024]{0,2,1:T(8,128)(2,1)} %bitcast.14), calls=%async_computation | async-start | bytes 8388608 | tf_op jit(solution)/shard_map/all_to_all | solution.py:17
  72.0 0.0 all-gather.8.cloned.1.call-start
  72.1 63.8 %all-to-all-done = bf16[128,16,1024]{0,2,1:T(8,128)(2,1)} async-done(((bf16[128,16,1024]{0,2,1:T(8,128)(2,1)}), bf16[128,16,1024]{0,2,1:T(8,128)(2,1)}, u32[]{:S(2)}, u32[]{:S(2)}) %all-to-all-start) | async-done | bytes 4194336 | tf_op jit(solution)/shard_map/all_to_all | solution.py:17
  135.9 6.4 %copy.12 = bf16[16,128,1024]{2,1,0:T(8,128)(2,1)} copy(bf16[16,128,1024]{1,2,0:T(8,128)(2,1)} %bitcast.1) | data formatting | bytes 8388608 | tf_op jit(solution)/shard_map/all_to_all | solution.py:17
  142.3 29.6 %all-gather.6.cloned.1.call-done = bf16[2048,2048]{1,0:T(8,128)(2,1)} async-done(((bf16[128,2048]{1,0:T(8,128)(2,1)}), bf16[2048,2048]{1,0:T(8,128)(2,1)}) %all-gather.6.cloned.1.call-update) | async-done | bytes 8388624 | tf_op jit(solution)/shard_map/all_gather | solution.py:20
  171.8 14.3 %multiply_convert_fusion = (bf16[1024,2048]{1,0:T(8,128)(2,1)}, f32[1024,2048]{1,0:T(8,128)S(1)}) fusion(bf16[2048,1024]{1,0:T(8,128)(2,1)} %bitcast.15, bf16[2048,2048]{1,0:T(8,128)(2,1)} %all-gather.6.cloned.1.call-done), kind=kOutput, calls=%fused_computation.3 | convolution fusion | flops 8594128896 | bytes 25165824 | tf_op jit(solution)/shard_map/dot_general | solution.py:18
  186.2 0.0 copy-start.1
  186.2 5.3 %fusion.2 = f32[1024,256]{1,0:T(8,128)S(1)} fusion(f32[1024,2048]{1,0:T(8,128)S(1)} %get-tuple-element.4, bf16[16384,256]{1,0:T(8,128)(2,1)} %param.9, s32[]{:T(128)S(6)} %select_n.8), kind=kOutput, calls=%fused_computation.4 | convolution fusion | flops 6444548096 | bytes 10485764 | tf_op jit(solution)/shard_map/dot_general | solution.py:33
  191.4 67.2 %all-reduce.4 = bf16[1024,256]{1,0:T(8,128)(2,1)} all-reduce(f32[1024,256]{1,0:T(8,128)S(1)} %fusion.2), channel_id=1, replica_groups=mesh['wide'=16,'narrow'=8] {'narrow'}, use_global_device_ids=true, to_apply=%region_0.0 | all-reduce | flops 262144 | bytes 1572864 | tf_op jit(solution)/shard_map/psum | solution.py:36
  258.6 0.0 all-gather.8.cloned.1.call-update
  258.6 0.0 all-reduce.3.cloned.1.call-start
  258.7 0.0 copy-done.1
  258.7 0.2 copy.10
  258.9 71.8 %all-gather.8.cloned.1.call-done = bf16[16384,256]{1,0:T(8,128)(2,1)} async-done(((bf16[1024,256]{1,0:T(8,128)(2,1)}), bf16[16384,256]{1,0:T(8,128)(2,1)}) %all-gather.8.cloned.1.call-update) | async-done | bytes 8388624 | tf_op jit(solution)/shard_map/all_gather | solution.py:37
  330.7 1.8 fusion.9
  332.4 0.0 all-reduce.3.cloned.1.call-update
  332.5 0.2 reduce-scatter.2.cloned.1.call-start
  332.7 0.0 copy-start
  332.7 2.3 mul.21
  335.0 0.0 copy-done
  335.0 8.5 %fusion.4 = f32[1024,256]{1,0:T(8,128)} fusion(f32[128,8,16,128]{3,2,1,0:T(8,128)S(1)} %bitcast.13, s32[1024,2048]{1,0:T(8,128)} %param.7, bf16[1024,2048]{1,0:T(8,128)(2,1)S(1)} %copy-done, bf16[16384,256]{1,0:T(8,128)(2,1)} %all-gather.8.cloned.1.call-done, s32[]{:T(128)S(6)} %select_n.8), kind=kOutput, calls=%fused_computation.6 | convolution fusion | flops 1084227584 | bytes 23068676 | tf_op jit(solution)/shard_map/dot_general | solution.py:48
  343.5 0.0 reduce-scatter.2.cloned.1.call-update
  343.5 133.1 %all-reduce.3.cloned.1.call-done = f32[256,256]{1,0:T(8,128)} async-done(((f32[256,256]{1,0:T(8,128)}), f32[256,256]{1,0:T(8,128)}) %all-reduce.3.cloned.1.call-update) | async-done | bytes 262160 | tf_op jit(solution)/shard_map/psum | solution.py:46
  476.7 39.7 %reduce-scatter.2.cloned.1.call-done = f32[128,256]{1,0:T(8,128)} async-done(((f32[1024,256]{1,0:T(8,128)}), f32[128,256]{1,0:T(8,128)}) %reduce-scatter.2.cloned.1.call-update) | async-done | bytes 131088 | tf_op jit(solution)/shard_map/reduce_scatter | solution.py:47
  516.4 1.7 copy.19
Async XLA Ops:
  7.2 58.2 %all-gather.4.cloned.1.call-start = ((), (), s32[]{:S(2)}) async-start(), calls=%async_computation.2 | async-start | bytes 4718592 | tf_op jit(solution)/shard_map/all_gather | solution.py:16
  9.3 162.6 %all-gather.6.cloned.1.call-start = ((), (), s32[]{:S(2)}) async-start(), calls=%async_computation.3 | async-start | bytes 8912896 | tf_op jit(solution)/shard_map/all_gather | solution.py:20
  65.3 70.6 %all-to-all-start = ((bf16[128,16,1024]{0,2,1:T(8,128)(2,1)}), bf16[128,16,1024]{0,2,1:T(8,128)(2,1)}, u32[]{:S(2)}, u32[]{:S(2)}) async-start(bf16[128,16,1024]{0,2,1:T(8,128)(2,1)} %bitcast.14), calls=%async_computation | async-start | bytes 8388608 | tf_op jit(solution)/shard_map/all_to_all | solution.py:17
  72.0 258.6 %all-gather.8.cloned.1.call-start = ((), (), s32[]{:S(2)}) async-start(), calls=%async_computation.4 | async-start | bytes 8912896 | tf_op jit(solution)/shard_map/all_gather | solution.py:37
  186.2 72.5 %copy-start.1 = (f32[1024,16]{0,1:T(8,128)S(1)}, f32[1024,16]{0,1:T(8,128)}, u32[]{:S(2)}) copy-start(f32[1024,16]{0,1:T(8,128)} %param.8) | copy-start | bytes 196612
  258.6 218.1 %all-reduce.3.cloned.1.call-start = ((), (), s32[]{:S(2)}) async-start(), calls=%async_computation.6 | async-start | bytes 524288 | tf_op jit(solution)/shard_map/psum | solution.py:46
  332.5 183.9 %reduce-scatter.2.cloned.1.call-start = ((), (), s32[]{:S(2)}) async-start(), calls=%async_computation.5 | async-start | bytes 1179648 | tf_op jit(solution)/shard_map/reduce_scatter | solution.py:47
  332.7 2.3 copy-start
Sparse Core Ops, SparseCore 0:
  10.2 55.0 all-gather.3
  67.7 104.0 all-gather.5
  258.7 71.8 all-gather.7
  335.8 140.7 all-reduce.2
  479.5 36.8 reduce-scatter.1
where the time goes:
time: 525 us
  waiting for transfers between devices  394 us (75%)
  blocking collectives  67.2 us (13%)
  matrix products  29.9 us (6%)
  between operations  13.8 us (3%)
  local copies, waits for them, and re-layouts  12.6 us (2%)
  starting transfers between devices  7.09 us (1%)
    psum x1, waiting for transfers between devices, body(): gram = lax.psum(gram_part, ('wide', 'narrow'))  133 us
    all_gather x1, waiting for transfers between devices, body(): product_full = lax.all_gather(product_own, 'wide', axis=0, tiled=True)  71.8 us
    psum x1, blocking collectives, body(): product_own = lax.psum(partial_value, 'narrow').astype(jnp.bfloat16)  67.2 us
    all_to_all x1, waiting for transfers between devices, body(): lax.all_to_all(full_features, 'wide', split_axis=1, concat_axis=0, tiled=...  63.8 us
    all_gather x1, waiting for transfers between devices, body(): full_features = lax.all_gather(activations, 'narrow', axis=1, tiled=True)  55.3 us
    reduce_scatter x1, waiting for transfers between devices, body(): lax.psum_scatter(jnp.dot(residual, product_cols, preferred_element_type=j...  39.7 us
    all_gather x1, waiting for transfers between devices, body(): lax.all_gather(activations, 'wide', axis=0, tiled=True)  29.6 us
    dot_general x1, matrix products, body(): lax.dot_general(row_operand, lax.all_gather(activations, 'wide', axis=0,...  14.3 us
  transfers between devices with their start and end apart: 6, of which 6 were waited for; matrix products, arithmetic and copies ran while one was open for 3% of the time, Pallas kernels for 0%

commit v1 on v0

v1 whole, which is shorter than its diff:
```python
import functools

import jax
import jax.numpy as jnp
from jax import lax
from jax.experimental import pallas as pl
from jax.experimental.pallas import tpu as pltpu
from jax.sharding import PartitionSpec as P

MESH = pl.DeviceIdType.MESH
F32 = jnp.float32
BF16 = jnp.bfloat16

TREES = {
    "A1": {"yp": [(0, 0), (1, 0), (2, 0), (1, 1), (2, 1), (3, 1)], "z": [(1, 0)]},
    "A2": {"yp": [(0, 0), (1, 0), (2, 0), (2, 1), (3, 1), (0, 1)], "z": [(2, 0)]},
    "B1": {"ym": [(0, 0), (3, 0), (2, 0), (3, 1), (2, 1), (1, 1)], "z": [(3, 0)]},
    "B2": {"ym": [(0, 0), (3, 0), (2, 0), (2, 1), (1, 1), (0, 1)], "z": [(2, 0)]},
    "Ca": {"z": [(0, 0), (1, 1), (2, 1), (3, 1)], "yp": [(0, 1), (1, 1)], "ym": [(0, 1)]},
    "Cb": {"z": [(0, 0), (1, 1), (2, 1), (3, 1)], "yp": [(0, 1)], "ym": [(0, 1), (3, 1)]},
}
DIRS = ("yp", "ym", "z")
LAG_OF_DEPTH = (0, 0, 1, 1, 2, 2, 2)

SLOTS = (
    (((0, 0, 0, 0), "A2"), ((0, 0, 0, 1), "B2"), ((0, 0, 1, 0), "Ca"), ((0, 0, 1, 1), "Cb")),
    (((3, 0, 0, 0), "A2"), ((1, 0, 0, 1), "B2"), ((0, 1, 0, 0), "Ca"),
     ((3, 0, 1, 0), "A2"), ((1, 0, 1, 1), "B2"), ((0, 1, 1, 0), "Cb")),
    (((3, 0, 0, 1), "A2"), ((1, 0, 0, 0), "B2"), ((0, 1, 0, 1), "Ca"),
     ((3, 0, 1, 1), "A1"), ((1, 0, 1, 0), "B1"), ((0, 1, 1, 1), "Cb")),
    (((2, 0, 0, 0), "A1"), ((2, 0, 0, 1), "B1"), ((2, 0, 1, 0), "A1"), ((2, 0, 1, 1), "B1")),
    (((3, 1, 0, 0), "A1"), ((1, 1, 0, 1), "B1"), ((3, 1, 1, 0), "A1"), ((1, 1, 1, 1), "B1")),
    (((3, 1, 0, 1), "A1"), ((1, 1, 0, 0), "B1"), ((3, 1, 1, 1), "A1"), ((1, 1, 1, 0), "B1")),
    (((2, 1, 0, 0), "A1"), ((2, 1, 0, 1), "B1"), ((2, 1, 1, 0), "Ca"), ((2, 1, 1, 1), "Cb")),
)
SUB = 32
HALF = 64
PIECE = 128


def step_from(role, direction):
    dy, dz = role
    if direction == "z":
        return (dy, 1 - dz)
    return ((dy + (1 if direction == "yp" else 3)) % 4, dz)


def depths(kind):
    depth = {(0, 0): 0}
    for _ in range(8):
        for direction, roles in TREES[kind].items():
            for role in roles:
                if role in depth:
                    target = step_from(role, direction)
                    if target not in depth:
                        depth[target] = depth[role] + 1
    return depth


def kernel(
    act, wt, codes, scales, rf,
    out_prod, out_gram, out_h,
    cols, rows, hacc, hout, res, cbuf, sbuf, rn,
    ypt, yrecv, yt, hrt, prod, prodrecv, gpart, grecv, gall,
    loc, csem, csend, rsem, rsend,
    yrs_r, yrs_s, yag_r, yag_s, ywd_r, ywd_s, prs_r, prs_s, grs_r, grs_s, gag_r, gag_s, osem,
):
    w = lax.axis_index("wide")
    n = lax.axis_index("narrow")
    c = w % 2
    zh = (w // 2) % 2
    x = w // 4
    zl = n // 4
    y = n % 4
    k = w // 2
    feats = cols.shape[2]
    half_feats = feats // 2
    rank = rf.shape[1]
    tokens = PIECE * 16

    def dev(x_, zh_, c_, zl_, y_):
        return (((x_ % 4) * 2 + zh_) * 2 + c_, zl_ * 4 + y_ % 4)

    partner = dev(x, zh, 1 - c, zl, y)
    right = dev(x + 1, zh, c, zl, y)
    left = dev(x + 3, zh, c, zl, y)
    across = dev(x, 1 - zh, c, zl, y)
    targets = {
        "yp": dev(x, zh, c, zl, y + 1),
        "ym": dev(x, zh, c, zl, y + 3),
        "z": dev(x, zh, c, 1 - zl, y),
    }

    def piece(dx, q, cc):
        return (((x + dx) % 4) * 2 + (1 - zh if q else zh)) * 2 + (1 - c if cc else c)

    own = cols.at[w]
    act_copy = pltpu.make_async_copy(act, own, loc.at[0])
    act_copy.start()
    rn_copy = pltpu.make_async_copy(rf.at[pl.ds(pl.multiple_of(n * feats, 128), feats)], rn, loc.at[1])
    rn_copy.start()
    s_copy = pltpu.make_async_copy(scales, sbuf, loc.at[2])
    s_copy.start()
    out_rows = res.shape[0]
    quarter = out_rows // 4
    wt_copies = []
    for i in range(4):
        sl = pl.ds(i * quarter, quarter)
        a = pltpu.make_async_copy(wt.at[sl], res.at[sl], loc.at[3 + i])
        b = pltpu.make_async_copy(codes.at[sl], cbuf.at[sl], loc.at[7 + i])
        a.start()
        b.start()
        wt_copies.append((a, b))

    barrier = pltpu.get_barrier_semaphore()
    for j in range(1, 8):
        pl.semaphore_signal(barrier, inc=1, device_id=(w, (n + j) % 8), device_id_type=MESH)
        pl.semaphore_signal(barrier, inc=1, device_id=(((k + j) % 8) * 2 + c, n), device_id_type=MESH)
    pl.semaphore_signal(barrier, inc=1, device_id=partner, device_id_type=MESH)
    act_copy.wait()
    pl.semaphore_wait(barrier, 15)

    def remote(src, dst, ssem, rsem_, to):
        cp = pltpu.make_async_remote_copy(src, dst, ssem, rsem_, device_id=to, device_id_type=MESH)
        cp.start()
        return cp

    def arrived(ref, sem):
        pltpu.make_async_copy(ref, ref, sem).wait()

    col_sends = []

    def col_part(p, sub):
        return cols.at[p, pl.ds(sub * SUB, SUB)]

    def col_send(p, sub, to):
        i = len(col_sends)
        ref = col_part(p, sub)
        remote(ref, ref, csend.at[i], csem.at[p, sub], to)
        col_sends.append(ref)

    def col_wait(p, sub):
        arrived(col_part(p, sub), csem.at[p, sub])

    for i in range(4):
        col_send(w, i, right)
        col_send(w, (i + 2) % 4, left)
        col_send(w, i, across)
        col_send(w, i, partner)

    def col_slot(s):
        mine = []
        if s == 0:
            pass
        elif s in (1, 4):
            q = int(s == 4)
            for i in range(2):
                mine.append((piece(3, q, 0), i, (right, partner)))
                mine.append((piece(1, q, 0), 2 + i, (left, partner)))
            if s == 1:
                for i in range(2):
                    mine.append((piece(0, 1, 0), i, (partner,)))
        elif s in (2, 5):
            q = int(s == 5)
            if s == 2:
                for i in range(2):
                    mine.append((piece(0, 1, 0), 2 + i, (partner,)))
            for i in range(2):
                mine.append((piece(3, q, 0), 2 + i, (partner,)))
                mine.append((piece(1, q, 0), i, (partner,)))
        elif s in (3, 6):
            q = int(s == 6)
            for i in range(4):
                mine.append((piece(2, q, 0), (0, 2, 1, 3)[i], (partner,)))
        for p, sub, to in mine:
            col_wait(p, sub)
            for t in to:
                col_send(p, sub, t)
        if s == 2:
            p = piece(0, 1, 0)
            for i in range(4):
                col_send(p, i, right)
                col_send(p, (i + 2) % 4, left)

    y_root = 2 * (x % 2) + zh
    zl_root = x // 2
    dy = (y + 4 - y_root) % 4
    dz = (zl + 2 - zl_root) % 2
    role = dz * 4 + dy
    is_root = role == 0

    def among(role_list):
        hit = role == role_list[0][1] * 4 + role_list[0][0]
        for a, b in role_list[1:]:
            hit = jnp.logical_or(hit, role == b * 4 + a)
        return hit

    passes = {kind: {d: among(r) for d, r in table.items()} for kind, table in TREES.items()}
    lag_is = {}
    for kind in TREES:
        by_lag = {}
        for r, d in depths(kind).items():
            by_lag.setdefault(LAG_OF_DEPTH[d], []).append(r)
        lag_is[kind] = {lag: among(r) for lag, r in by_lag.items()}

    def row_part(p, tok):
        return rows.at[p, pl.ds(tok, SUB)]

    def col_half_part(p, tok):
        return cols.at[p, pl.ds(tok, SUB), pl.ds(pl.multiple_of(c * half_feats, 128), half_feats)]

    def root_take(s):
        for (dx, q, cc, h), _ in SLOTS[s]:
            if cc:
                p = piece(dx, q, 1)
                col_wait(p, 2 * h)
                col_wait(p, 2 * h + 1)

        @pl.when(is_root)
        def _():
            for (dx, q, cc, h), _ in SLOTS[s]:
                p = piece(dx, q, cc)
                for i in range(2):
                    pltpu.make_async_copy(
                        col_half_part(p, h * HALF + i * SUB), row_part(p, h * HALF + i * SUB), rsem.at[p, 2 * h + i]
                    ).start()

    def row_slot(s):
        for lag in (2, 1, 0):
            m = s - lag
            if not 0 <= m < len(SLOTS):
                continue

            @pl.loop(0, 2)
            def _(i, m=m, lag=lag):
                for (dx, q, cc, h), kind in SLOTS[m]:
                    if lag not in lag_is[kind]:
                        continue

                    @pl.when(lag_is[kind][lag])
                    def _(dx=dx, q=q, cc=cc, h=h, kind=kind):
                        p = piece(dx, q, cc)
                        ref = row_part(p, pl.multiple_of(h * HALF + i * SUB, SUB))
                        sem = rsem.at[p, 2 * h + i]
                        arrived(ref, sem)
                        for d, hit in passes[kind].items():

                            @pl.when(hit)
                            def _(d=d):
                                remote(ref, ref, rsend.at[DIRS.index(d), p, h], sem, targets[d])

    def row_drain():
        for slot in SLOTS:
            for (dx, q, cc, h), kind in slot:
                for d, hit in passes[kind].items():

                    @pl.when(hit)
                    def _(dx=dx, q=q, cc=cc, h=h, d=d):
                        p = piece(dx, q, cc)
                        arrived(rows.at[p, pl.ds(h * HALF, HALF)], rsend.at[DIRS.index(d), p, h])

    blocks = 4
    block = hacc.shape[0] // blocks

    def hessian(dx, q, first=False, last=False):
        kk = ((x + dx) % 4) * 2 + (1 - zh if q else zh)

        @pl.loop(0, blocks)
        def _(b):
            off = pl.multiple_of(b * block, block)
            left_ = rows[pl.ds(2 * kk, 2), :, pl.ds(off, block)].reshape(2 * PIECE, block)
            right_ = cols[pl.ds(2 * kk, 2)].reshape(2 * PIECE, feats)
            part = lax.dot_general(left_, right_, (((0,), (0,)), ((), ())), preferred_element_type=F32)
            sl = pl.ds(off, block)
            if first:
                hacc[sl] = part
            elif last:
                hout[sl] = ((hacc[sl] + part) * (1.0 / tokens)).astype(BF16)
                pltpu.make_async_copy(hout.at[sl], out_h.at[sl], osem.at[b]).start()
            else:
                hacc[sl] += part

    def residual(i):
        a, b = wt_copies[i]
        a.wait()
        b.wait()
        step = 64

        @pl.loop(0, quarter // step)
        def _(j):
            sl = pl.ds(pl.multiple_of(i * quarter + j * step, step), step)
            for g in range(feats // 128):
                lanes = pl.ds(g * 128, 128)
                value = cbuf[sl, lanes].astype(F32) * sbuf[sl, g : g + 1]
                res[sl, lanes] = (res[sl, lanes].astype(F32) - value).astype(BF16)

    rn_copy.wait()
    ypt[...] = jnp.dot(cols[w], rn[...], preferred_element_type=F32).T
    share = rank // 8

    def narrow_block(ref, who):
        return ref.at[pl.ds(pl.multiple_of(who * share, share), share)]

    for j in range(1, 8):
        to = (n + j) % 8
        remote(narrow_block(ypt, to), yrecv.at[n], yrs_s.at[to], yrs_r.at[n], (w, to))
    yrecv[n] = ypt[pl.ds(pl.multiple_of(n * share, share), share)]

    root_take(0)
    row_slot(0)
    s_copy.wait()
    residual(0)

    for j in range(1, 8):
        who = (n + j) % 8
        arrived(yrecv.at[who], yrs_r.at[who])
    total = yrecv[0]
    for j in range(1, 8):
        total += yrecv[j]
    lanes_w = pl.ds(pl.multiple_of(w * PIECE, PIECE), PIECE)
    yt[pl.ds(pl.multiple_of(n * share, share), share), lanes_w] = total.astype(BF16)

    def y_block(who):
        return yt.at[pl.ds(pl.multiple_of(who * share, share), share), lanes_w]

    for j in range(1, 8):
        to = (n + j) % 8
        remote(y_block(n), y_block(n), yag_s.at[to], yag_r.at[n], (w, to))

    residual(1)
    col_slot(1)
    root_take(1)
    row_slot(1)

    for j in range(1, 8):
        who = (n + j) % 8
        arrived(y_block(who), yag_r.at[who])

    def y_piece(p):
        return yt.at[:, pl.ds(pl.multiple_of(p * PIECE, PIECE), PIECE)]

    for j in range(1, 8):
        to = (k + j) % 8
        remote(y_piece(w), y_piece(w), ywd_s.at[j], ywd_r.at[w], (2 * to + c, n))
    remote(y_piece(w), y_piece(w), ywd_s.at[0], ywd_r.at[w], partner)

    residual(2)
    col_slot(2)
    root_take(2)
    row_slot(2)
    hessian(0, 0, first=True)
    residual(3)
    col_slot(3)
    root_take(3)
    row_slot(3)
    for j in range(1, 8):
        p = ((k + j) % 8) * 2 + c
        arrived(y_piece(p), ywd_r.at[p])
        remote(y_piece(p), y_piece(p), ywd_s.at[7 + j], ywd_r.at[p], partner)
    col_slot(4)
    root_take(4)
    row_slot(4)
    hessian(3, 0)
    hessian(1, 0)
    col_slot(5)
    root_take(5)
    row_slot(5)
    hessian(0, 1)
    hessian(2, 0)
    for j in range(8):
        p = ((k + j) % 8) * 2 + 1 - c
        arrived(y_piece(p), ywd_r.at[p])
    col_slot(6)
    root_take(6)
    row_slot(6)

    hblock = 512

    @pl.loop(0, feats // hblock)
    def _(b):
        lanes = pl.ds(pl.multiple_of(b * hblock, hblock), hblock)
        value = jnp.dot(yt[...], cols[:, :, lanes].reshape(tokens, hblock), preferred_element_type=F32)
        hrt[:, lanes] = (value * (1.0 / tokens)).astype(BF16)

    row_slot(7)

    @pl.loop(0, 4)
    def _(b):
        sl = pl.ds(pl.multiple_of(b * quarter, quarter), quarter)
        prod[sl] = lax.dot_general(res[sl], hrt[...], (((1,), (1,)), ((), ())), preferred_element_type=F32)

    own_rows = out_rows // 8

    def prod_block(who):
        return prod.at[pl.ds(pl.multiple_of(who * own_rows, own_rows), own_rows)]

    for j in range(1, 8):
        to = (n + j) % 8
        remote(prod_block(to), prodrecv.at[n], prs_s.at[to], prs_r.at[n], (w, to))
    gpart[...] = jnp.dot(hrt[...], rn[...], preferred_element_type=F32)
    for j in range(1, 8):
        to = (n + j) % 8
        remote(narrow_block(gpart, to), grecv.at[n], grs_s.at[to], grs_r.at[n], (w, to))
    grecv[n] = gpart[pl.ds(pl.multiple_of(n * share, share), share)]
    prodrecv[n] = prod[pl.ds(pl.multiple_of(n * own_rows, own_rows), own_rows)]

    row_slot(8)
    hessian(3, 1)
    for j in range(1, 8):
        who = (n + j) % 8
        arrived(grecv.at[who], grs_r.at[who])
    gsum = grecv[0]
    for j in range(1, 8):
        gsum += grecv[j]
    gall[pl.ds(pl.multiple_of(n * share, share), share)] = gsum
    for j in range(1, 8):
        to = (n + j) % 8
        remote(narrow_block(gall, n), narrow_block(gall, n), gag_s.at[to], gag_r.at[n], (w, to))
    hessian(1, 1)
    hessian(2, 1, last=True)

    for j in range(1, 8):
        who = (n + j) % 8
        arrived(prodrecv.at[who], prs_r.at[who])
    psum = prodrecv[0]
    for j in range(1, 8):
        psum += prodrecv[j]
    out_prod[...] = psum
    for j in range(1, 8):
        who = (n + j) % 8
        arrived(narrow_block(gall, who), gag_r.at[who])
    out_gram[...] = gall[...].T

    for i, ref in enumerate(col_sends):
        arrived(ref, csend.at[i])
    row_drain()
    for j in range(1, 8):
        to = (n + j) % 8
        arrived(narrow_block(ypt, to), yrs_s.at[to])
        arrived(y_block(n), yag_s.at[to])
        arrived(prod_block(to), prs_s.at[to])
        arrived(narrow_block(gpart, to), grs_s.at[to])
        arrived(narrow_block(gall, n), gag_s.at[to])
    for j in range(15):
        arrived(y_piece(w), ywd_s.at[j])
    for b in range(blocks):
        sl = pl.ds(b * block, block)
        pltpu.make_async_copy(hout.at[sl], out_h.at[sl], osem.at[b]).wait()


def body(activations, weight_tile, codes, group_scales, right_factor):
    piece_tokens, feats = activations.shape
    out_rows = weight_tile.shape[0]
    rank = right_factor.shape[1]
    assert piece_tokens == PIECE
    dma = pltpu.SemaphoreType.DMA
    any_spec = pl.BlockSpec(memory_space=pl.ANY)
    vmem_spec = pl.BlockSpec(memory_space=pltpu.VMEM)
    return pl.pallas_call(
        kernel,
        out_shape=(
            jax.ShapeDtypeStruct((out_rows // 8, rank), F32),
            jax.ShapeDtypeStruct((rank, rank), F32),
            jax.ShapeDtypeStruct((out_rows, feats), BF16),
        ),
        in_specs=[any_spec] * 5,
        out_specs=(vmem_spec, vmem_spec, any_spec),
        scratch_shapes=[
            pltpu.VMEM((16, PIECE, feats), BF16),
            pltpu.VMEM((16, PIECE, feats // 2), BF16),
            pltpu.VMEM((out_rows, feats), F32),
            pltpu.VMEM((out_rows, feats), BF16),
            pltpu.VMEM((out_rows, feats), BF16),
            pltpu.VMEM((out_rows, feats), jnp.int32),
            pltpu.VMEM((out_rows, group_scales.shape[1]), F32),
            pltpu.VMEM((feats, rank), BF16),
            pltpu.VMEM((rank, PIECE), F32),
            pltpu.VMEM((8, rank // 8, PIECE), F32),
            pltpu.VMEM((rank, 16 * PIECE), BF16),
            pltpu.VMEM((rank, feats), BF16),
            pltpu.VMEM((out_rows, rank), F32),
            pltpu.VMEM((8, out_rows // 8, rank), F32),
            pltpu.VMEM((rank, rank), F32),
            pltpu.VMEM((8, rank // 8, rank), F32),
            pltpu.VMEM((rank, rank), F32),
            dma((11,)),
            dma((16, 4)),
            dma((64,)),
            dma((16, 4)),
            dma((3, 16, 2)),
            dma((8,)), dma((8,)), dma((8,)), dma((8,)), dma((16,)), dma((15,)),
            dma((8,)), dma((8,)), dma((8,)), dma((8,)), dma((8,)), dma((8,)),
            dma((4,)),
        ],
        compiler_params=pltpu.CompilerParams(
            collective_id=0, has_side_effects=True, vmem_limit_bytes=62 << 20
        ),
    )(activations, weight_tile, codes, group_scales, right_factor)


def solution(mesh):
    spec = P("wide", "narrow")
    return jax.shard_map(
        body,
        mesh=mesh,
        in_specs=(spec, spec, spec, spec, P()),
        out_specs=(P(("wide", "narrow"), None), P(), spec),
        check_vma=False,
    )
```

time: 525 us -> 227 us (0.43)
  waiting for transfers between devices: 394 us -> 0 us
  Pallas kernels: 0 us -> 216 us
  blocking collectives: 67.2 us -> 0 us
  matrix products: 29.9 us -> 0 us
  between operations: 13.8 us -> 0.64 us
  starting transfers between devices: 7.09 us -> 0 us
    pallas_call x0 -> x1, Pallas kernels: none -> 216 us  [body(): pl.pallas_call(kernel, out_shape=(jax.ShapeDtypeStruct((out_rows // 8, ra...]
    all_gather x3 -> x0, waiting for transfers between devices: 157 us -> none  [the longest x1 71.8 us: body(): product_full = lax.all_gather(product_own, 'wide', axis=0, tiled=True)]
    psum x1 -> x0, waiting for transfers between devices: 133 us -> none  [body(): gram = lax.psum(gram_part, ('wide', 'narrow'))]
    psum x1 -> x0, blocking collectives: 67.2 us -> none  [body(): product_own = lax.psum(partial_value, 'narrow').astype(jnp.bfloat16)]
    all_to_all x1 -> x0, waiting for transfers between devices: 63.8 us -> none  [body(): lax.all_to_all(full_features, 'wide', split_axis=1, concat_axis=0, tiled=...]
    reduce_scatter x1 -> x0, waiting for transfers between devices: 39.7 us -> none  [body(): lax.psum_scatter(jnp.dot(residual, product_cols, preferred_element_type=j...]
    dot_general x4 -> x0, matrix products: 29.9 us -> none  [the longest x1 14.3 us: body(): lax.dot_general(row_operand, lax.all_gather(activations, 'wide', axis=0,...]
    all_to_all x1 -> x0, starting transfers between devices: 6.7 us -> none  [body(): lax.all_to_all(full_features, 'wide', split_axis=1, concat_axis=0, tiled=...]
  transfers between devices with their start and end apart: 6 -> 0, of which waited for: 6 -> 0; matrix products, arithmetic and copies ran while one was open for 3% -> 0% of each run, Pallas kernels for 0% -> 0%
where the time goes in v1:
time: 227 us
  Pallas kernels  216 us (95%)
  local copies, waits for them, and re-layouts  9.86 us (4%)
    pallas_call x1, Pallas kernels, body(): pl.pallas_call(kernel, out_shape=(jax.ShapeDtypeStruct((out_rows // 8, ra...  216 us
    unnamed x4, local copies, waits for them, and re-layouts  9.86 us

profile of v1, /device:TPU:0, one launch (start us, length us, event | category | flops | bytes accessed | tf_op | source)
XLA Modules:
  0.0 226.6 jit_solution(6214359506996626185)
XLA Ops:
  0.6 1.8 copy.8.scales
  2.5 216.1 %shard_map.76 = (f32[128,256]{1,0:T(8,128)}, f32[256,256]{1,0:T(8,128)}, bf16[1024,2048]{1,0:T(8,128)(2,1)}) custom-call(bf16[128,2048]{1,0:T(8,128)(2,1)} %act.1, bf16[1024,2048]{1,0:T(8,128)(2,1)} %wt.1, s32[1024,2048]{1,0:T(8,128)} %codes.1, f32[1024,16]{1,0:T(8,128)} %copy.8.scales, bf16[16384,256]{1,0:T(8,128)(2,1)} %rf.1), custom_call_target="tpu_custom_call" | custom-call | tf_op jit(solution)/shard_map/pallas_call | solution.py:459
  218.5 1.6 copy.12
  220.1 1.7 copy.13
  221.8 4.8 %copy.14 = bf16[1024,2048]{1,0:T(8,128)(2,1)} copy(bf16[1024,2048]{1,0:T(8,128)(2,1)} %get-tuple-element.8) | data formatting | bytes 8388608

commit v2 on v0

v2 whole, which is shorter than its diff:
```python
import jax
import jax.numpy as jnp
from jax import lax
from jax.experimental import pallas as pl
from jax.experimental.pallas import tpu as pltpu
from jax.sharding import PartitionSpec as P

MESH = pl.DeviceIdType.MESH
F32 = jnp.float32
BF16 = jnp.bfloat16
DIRS = ("yp", "ym", "z")
SUB = 32
PIECE = 128

PLAN = (
    ("c", 0, 0, 0),
    ("c", 0, 0, 1),
    ("c", 0, 0, 2),
    ("c", 0, 0, 3),
    ("ydot",),
    ("r", 768, 0, 0, 0, 0, 0, 0, 0),
    ("r", 784, 0, 0, 0, 0, 0, 0, 0),
    ("r", 672, 0, 0, 0, 0, 0, 0, 0),
    ("r", 688, 0, 0, 0, 0, 0, 0, 0),
    ("o", 0, 0, 0),
    ("o", 0, 0, 1),
    ("res", 0),
    ("o", 0, 0, 2),
    ("r", 584, 0, 0, 0, 0, 0, 0, 0),
    ("o", 0, 0, 3),
    ("r", 792, 0, 0, 0, 0, 0, 0, 0),
    ("res", 1),
    ("r", 680, 0, 0, 0, 0, 0, 0, 0),
    ("r", 824, 0, 0, 0, 0, 0, 0, 0),
    ("c", 3, 0, 0),
    ("c", 1, 0, 2),
    ("res", 2),
    ("r", 643, 0, 0, 672, 0, 0, 0, 0),
    ("r", 609, 0, 0, 0, 0, 0, 0, 0),
    ("c", 0, 1, 0),
    ("res", 3),
    ("o", 3, 0, 0),
    ("o", 1, 0, 2),
    ("r", 644, 840, 0, 944, 0, 0, 0, 0),
    ("r", 651, 0, 0, 0, 0, 0, 0, 0),
    ("o", 0, 1, 0),
    ("r", 681, 0, 0, 0, 0, 0, 0, 0),
    ("c", 3, 0, 1),
    ("c", 1, 0, 3),
    ("r", 588, 0, 928, 680, 0, 0, 0, 0),
    ("r", 787, 0, 0, 0, 0, 0, 0, 0),
    ("r", 625, 0, 0, 0, 0, 0, 0, 0),
    ("c", 0, 1, 1),
    ("r", 788, 609, 0, 0, 0, 0, 0, 0),
    ("o", 3, 0, 1),
    ("o", 1, 0, 3),
    ("r", 667, 0, 584, 899, 0, 0, 0, 0),
    ("r", 633, 0, 0, 0, 0, 0, 0, 0),
    ("o", 0, 1, 1),
    ("r", 668, 0, 688, 0, 0, 0, 0, 0),
    ("c", 3, 0, 2),
    ("c", 1, 0, 0),
    ("r", 803, 544, 865, 900, 0, 0, 0, 0),
    ("r", 769, 844, 0, 0, 0, 0, 0, 0),
    ("c", 0, 1, 2),
    ("r", 612, 0, 936, 0, 0, 0, 0, 0),
    ("o", 3, 0, 2),
    ("o", 1, 0, 0),
    ("r", 619, 881, 0, 520, 0, 0, 0, 0),
    ("r", 585, 0, 0, 651, 0, 0, 0, 0),
    ("o", 0, 1, 2),
    ("r", 684, 560, 643, 0, 0, 0, 0, 0),
    ("c", 3, 0, 3),
    ("c", 1, 0, 1),
    ("r", 627, 889, 588, 545, 0, 0, 0, 0),
    ("r", 657, 552, 0, 937, 0, 0, 0, 0),
    ("c", 0, 1, 3),
    ("Q",),
    ("r", 628, 0, 644, 0, 0, 0, 0, 0),
    ("yred",),
    ("o", 3, 0, 3),
    ("r", 0, 0, 625, 0, 0, 0, 0, 0),
    ("o", 1, 0, 1),
    ("r", 699, 868, 0, 923, 704, 0, 0, 0),
    ("o", 0, 1, 3),
    ("r", 601, 515, 907, 524, 0, 584, 672, 688),
    ("r", 636, 619, 0, 0, 0, 0, 0, 0),
    ("c", 2, 0, 0),
    ("c", 2, 0, 2),
    ("r", 578, 516, 633, 924, 720, 588, 609, 643),
    ("r", 802, 841, 681, 561, 728, 672, 688, 644),
    ("r", 0, 0, 612, 940, 0, 625, 584, 0),
    ("r", 0, 0, 0, 0, 0, 0, 680, 0),
    ("c", 2, 0, 1),
    ("c", 2, 0, 3),
    ("r", 658, 523, 667, 569, 760, 633, 643, 609),
    ("r", 818, 883, 875, 913, 0, 0, 588, 681),
    ("r", 0, 628, 668, 0, 0, 0, 651, 0),
    ("r", 0, 553, 0, 0, 0, 0, 0, 0),
    ("o", 2, 0, 0),
    ("r", 650, 0, 0, 0, 0, 0, 0, 0),
    ("o", 2, 0, 2),
    ("r", 810, 0, 0, 0, 0, 0, 0, 0),
    ("o", 2, 0, 1),
    ("r", 794, 0, 0, 548, 0, 0, 0, 0),
    ("o", 2, 0, 3),
    ("r", 698, 0, 585, 955, 672, 688, 644, 584),
    ("r", 0, 0, 0, 0, 723, 612, 625, 0),
    ("c", 3, 1, 0),
    ("c", 1, 1, 2),
    ("r", 583, 539, 684, 555, 609, 832, 619, 667),
    ("r", 805, 857, 627, 914, 0, 680, 681, 768),
    ("r", 0, 0, 0, 0, 0, 0, 0, 588),
    ("o", 3, 1, 0),
    ("r", 0, 0, 0, 0, 724, 0, 633, 0),
    ("o", 1, 1, 2),
    ("r", 655, 540, 657, 521, 520, 585, 0, 668),
    ("r", 685, 0, 884, 0, 0, 784, 0, 912),
    ("r", 0, 0, 0, 0, 0, 643, 0, 0),
    ("yag",),
    ("r", 0, 892, 0, 906, 560, 0, 667, 625),
    ("r", 0, 0, 0, 0, 739, 0, 0, 0),
    ("c", 3, 1, 1),
    ("c", 1, 1, 3),
    ("r", 599, 556, 699, 512, 680, 627, 612, 684),
    ("r", 693, 512, 601, 563, 524, 856, 668, 792),
    ("r", 0, 578, 658, 954, 705, 651, 768, 619),
    ("r", 0, 528, 636, 528, 0, 601, 628, 657),
    ("r", 0, 529, 0, 564, 0, 824, 0, 952),
    ("r", 0, 839, 0, 911, 0, 644, 0, 633),
    ("c", 3, 1, 2),
    ("c", 1, 1, 0),
    ("r", 615, 571, 650, 537, 515, 851, 784, 699),
    ("r", 581, 599, 834, 685, 738, 681, 585, 544),
    ("r", 0, 530, 512, 0, 0, 636, 627, 612),
    ("r", 0, 0, 698, 0, 0, 0, 684, 0),
    ("o", 3, 1, 1),
    ("r", 799, 0, 0, 0, 561, 545, 0, 658),
    ("r", 0, 0, 0, 0, 754, 0, 0, 787),
    ("r", 0, 0, 0, 0, 651, 0, 0, 0),
    ("o", 1, 1, 3),
    ("r", 637, 0, 583, 572, 0, 667, 0, 0),
    ("o", 3, 1, 2),
    ("r", 623, 0, 0, 0, 0, 0, 0, 0),
    ("o", 1, 1, 0),
    ("r", 589, 536, 0, 693, 0, 0, 0, 628),
    ("c", 3, 1, 3),
    ("c", 1, 1, 1),
    ("r", 695, 615, 528, 536, 619, 788, 792, 916),
    ("r", 789, 522, 655, 514, 746, 583, 657, 0),
    ("r", 0, 0, 855, 0, 0, 0, 578, 0),
    ("ya",),
    ("r", 0, 568, 941, 568, 516, 668, 601, 585),
    ("r", 0, 570, 0, 519, 569, 867, 824, 650),
    ("r", 0, 837, 0, 0, 730, 0, 0, 803),
    ("o", 3, 1, 3),
    ("r", 0, 0, 0, 0, 0, 684, 0, 0),
    ("o", 1, 1, 1),
    ("r", 0, 531, 0, 0, 553, 0, 0, 627),
    ("c", 2, 1, 0),
    ("c", 2, 1, 2),
    ("r", 703, 637, 949, 695, 548, 769, 699, 698),
    ("r", 582, 527, 536, 531, 741, 657, 787, 552),
    ("r", 806, 0, 871, 535, 539, 0, 599, 578),
    ("r", 669, 0, 0, 0, 0, 0, 0, 0),
    ("yn", 3, 0),
    ("r", 0, 532, 0, 0, 0, 0, 636, 0),
    ("yn", 1, 0),
    ("r", 0, 879, 568, 532, 628, 866, 658, 897),
    ("r", 0, 557, 531, 547, 540, 699, 685, 655),
    ("r", 0, 547, 0, 959, 521, 882, 583, 601),
    ("r", 0, 565, 0, 551, 735, 0, 693, 802),
    ("r", 0, 845, 0, 0, 556, 0, 788, 599),
    ("c", 2, 1, 1),
    ("c", 2, 1, 3),
    ("o", 2, 1, 0),
    ("r", 654, 513, 0, 0, 0, 0, 0, 0),
    ("o", 2, 1, 2),
    ("r", 662, 838, 581, 513, 563, 658, 803, 636),
    ("r", 630, 0, 0, 925, 725, 555, 650, 523),
    ("r", 814, 0, 0, 0, 529, 581, 615, 0),
    ("o", 2, 1, 1),
    ("r", 0, 546, 0, 0, 0, 0, 0, 0),
    ("yn", 3, 1),
    ("yn", 1, 1),
    ("r", 0, 0, 0, 0, 0, 0, 0, 818),
    ("o", 2, 1, 3),
    ("r", 798, 0, 951, 546, 578, 810, 802, 0),
    ("r", 702, 0, 532, 0, 742, 0, 698, 0),
    ("yf", 0),
    ("r", 0, 562, 893, 662, 571, 693, 818, 583),
    ("r", 0, 630, 0, 0, 537, 623, 769, 938),
    ("r", 0, 0, 0, 0, 750, 858, 0, 0),
    ("r", 0, 0, 0, 0, 0, 685, 0, 0),
    ("yf", 1),
    ("r", 0, 0, 547, 517, 530, 589, 0, 703),
    ("r", 0, 0, 703, 0, 0, 650, 0, 0),
    ("r", 0, 0, 623, 0, 0, 0, 0, 0),
    ("yoth",),
    ("r", 0, 567, 669, 654, 0, 869, 695, 669),
    ("r", 0, 0, 0, 562, 0, 0, 581, 615),
    ("r", 0, 0, 0, 0, 0, 0, 655, 0),
    ("hr", 0),
    ("r", 0, 554, 546, 573, 734, 582, 0, 794),
    ("r", 0, 0, 589, 0, 599, 0, 0, 0),
    ("r", 0, 0, 0, 0, 572, 0, 0, 0),
    ("r", 0, 0, 0, 0, 693, 0, 0, 0),
    ("hr", 1),
    ("r", 0, 538, 918, 554, 0, 698, 637, 805),
    ("r", 0, 0, 562, 958, 0, 564, 623, 0),
    ("r", 0, 0, 0, 0, 0, 0, 810, 0),
    ("hr", 2),
    ("r", 0, 0, 582, 559, 519, 0, 0, 581),
    ("hr", 3),
    ("r", 0, 549, 513, 538, 522, 799, 794, 927),
    ("r", 0, 541, 886, 0, 0, 655, 703, 0),
    ("r", 0, 575, 910, 0, 0, 0, 0, 0),
    ("prod", 1),
    ("r", 0, 0, 554, 525, 615, 695, 669, 789),
    ("r", 0, 0, 0, 0, 685, 853, 589, 0),
    ("prod", 0),
    ("r", 0, 534, 702, 549, 570, 0, 662, 702),
    ("r", 0, 543, 0, 518, 517, 0, 805, 623),
    ("r", 0, 0, 0, 0, 0, 0, 0, 637),
    ("r", 0, 0, 0, 0, 0, 0, 0, 806),
    ("prod", 2),
    ("r", 0, 0, 538, 543, 0, 870, 799, 0),
    ("r", 0, 0, 0, 0, 0, 514, 630, 0),
    ("r", 0, 0, 0, 0, 0, 669, 0, 0),
    ("prod", 3),
    ("r", 0, 533, 0, 566, 527, 0, 582, 942),
    ("r", 0, 526, 0, 533, 559, 0, 0, 589),
    ("gram",),
    ("r", 0, 0, 549, 0, 695, 814, 702, 0),
    ("r", 0, 0, 0, 0, 0, 703, 654, 0),
    ("r", 0, 0, 0, 0, 0, 0, 789, 0),
    ("H", 0, 0, 0, 1, 0, 1),
    ("r", 0, 574, 0, 550, 637, 662, 806, 926),
    ("r", 0, 550, 0, 0, 0, 0, 0, 0),
    ("H", 0, 0, 0, 1, 1, 1),
    ("r", 0, 0, 543, 558, 541, 798, 814, 565),
    ("r", 0, 0, 0, 0, 525, 0, 0, 582),
    ("H", 1, 0, 3, 0, 0, 0),
    ("r", 0, 558, 533, 542, 0, 535, 0, 630),
    ("r", 0, 0, 0, 0, 0, 702, 0, 557),
    ("prodsend", 4),
    ("prodsend", 3),
    ("r", 0, 0, 0, 0, 0, 0, 798, 0),
    ("prodsend", 5),
    ("r", 0, 0, 0, 0, 0, 551, 0, 0),
    ("H", 1, 0, 3, 0, 1, 0),
    ("r", 0, 542, 550, 0, 518, 654, 0, 567),
    ("r", 0, 0, 0, 0, 662, 0, 0, 0),
    ("prodsend", 7),
    ("r", 0, 0, 0, 0, 575, 0, 0, 0),
    ("prodsend", 2),
    ("prodsend", 6),
    ("prodsend", 1),
    ("r", 0, 0, 558, 0, 0, 573, 0, 0),
    ("H", 2, 0, 1, 1, 0, 0),
    ("r", 0, 0, 0, 0, 630, 0, 0, 0),
    ("H", 2, 0, 1, 1, 1, 0),
    ("gramred",),
    ("r", 0, 0, 542, 0, 654, 566, 0, 534),
    ("r", 0, 0, 0, 0, 574, 0, 0, 526),
    ("H", 3, 1, 2, 1, 0, -1),
    ("H", 3, 1, 2, 1, 1, -1),
)

def kernel(
    act, wt, codes, scales, rf,
    out_prod, out_gram, out_h,
    cols, rows, hacc, res, cbuf, sbuf, scol, rn,
    ypt, yrecv, yt, hrt, prod, prodrecv, gpart, grecv, gall,
    loc, csem, csend, rsem, rsend,
    yrs_r, yrs_s, yag_r, yag_s, ywd_r, ywd_s, prs_r, prs_s, grs_r, grs_s, gag_r, gag_s,
):
    w = lax.axis_index("wide")
    n = lax.axis_index("narrow")
    c = lax.rem(w, 2)
    k = lax.div(w, 2)
    zh = lax.rem(k, 2)
    x = lax.div(k, 2)
    zl = lax.div(n, 4)
    y = lax.rem(n, 4)
    feats = cols.shape[2]
    half_feats = feats // 2
    rank = rf.shape[1]
    tokens = PIECE * 16

    def dev(x_, zh_, c_, zl_, y_):
        return ((lax.rem(x_, 4) * 2 + zh_) * 2 + c_, zl_ * 4 + lax.rem(y_, 4))

    partner = dev(x, zh, 1 - c, zl, y)
    right = dev(x + 1, zh, c, zl, y)
    left = dev(x + 3, zh, c, zl, y)
    across = dev(x, 1 - zh, c, zl, y)
    targets = {
        "yp": dev(x, zh, c, zl, y + 1),
        "ym": dev(x, zh, c, zl, y + 3),
        "z": dev(x, zh, c, 1 - zl, y),
    }

    def peer(j):
        return lax.rem(n + j, 8)

    def piece(dx, q, cc):
        return (lax.rem(x + dx, 4) * 2 + lax.rem(zh + q, 2)) * 2 + lax.rem(c + cc, 2)

    act_copy = pltpu.make_async_copy(act, cols.at[w], loc.at[0])
    act_copy.start()
    rn_copy = pltpu.make_async_copy(rf.at[pl.ds(pl.multiple_of(n * feats, 128), feats)], rn, loc.at[1])
    rn_copy.start()
    s_copy = pltpu.make_async_copy(scales, sbuf, loc.at[2])
    s_copy.start()
    out_rows = res.shape[0]
    quarter = out_rows // 4
    wt_copies = []
    for i in range(4):
        sl = pl.ds(i * quarter, quarter)
        a = pltpu.make_async_copy(wt.at[sl], res.at[sl], loc.at[3 + i])
        b = pltpu.make_async_copy(codes.at[sl], cbuf.at[sl], loc.at[7 + i])
        a.start()
        b.start()
        wt_copies.append((a, b))

    barrier = pltpu.get_barrier_semaphore()
    for j in range(1, 8):
        pl.semaphore_signal(barrier, inc=1, device_id=(w, peer(j)), device_id_type=MESH)
        pl.semaphore_signal(barrier, inc=1, device_id=(lax.rem(k + j, 8) * 2 + c, n), device_id_type=MESH)
    pl.semaphore_signal(barrier, inc=1, device_id=partner, device_id_type=MESH)
    act_copy.wait()
    pl.semaphore_wait(barrier, 15)

    def remote(src, dst, ssem, rsem_, to):
        pltpu.make_async_remote_copy(src, dst, ssem, rsem_, device_id=to, device_id_type=MESH).start()

    def arrived(ref, sem):
        pltpu.make_async_copy(ref, ref, sem).wait()

    col_sends = []

    def col_part(p, sub):
        return cols.at[p, pl.ds(sub * SUB, SUB)]

    def col_send(p, sub, to):
        ref = col_part(p, sub)
        remote(ref, ref, csend.at[0], csem.at[p, sub], to)
        col_sends.append(ref)

    for i in range(4):
        col_send(w, i, right)
        col_send(w, (i + 2) % 4, left)
        col_send(w, i, across)
        col_send(w, i, partner)

    dy = lax.rem(y + 4 - (2 * lax.rem(x, 2) + zh), 4)
    dz = lax.rem(zl + 2 - lax.div(x, 2), 2)
    role = dz * 4 + dy
    is_role = [role == r for r in range(8)]
    role_one = [jnp.where(hit, 1, 0) for hit in is_role]

    def root_take(p, sub):
        @pl.when(is_role[0])
        def _():
            src = cols.at[p, pl.ds(sub * SUB, SUB), pl.ds(pl.multiple_of(c * half_feats, 128), half_feats)]
            pltpu.make_async_copy(src, rows.at[p, pl.ds(sub * SUB, SUB)], rsem.at[p, sub]).start()

    def row_step(entries):
        code = sum(entry * one for entry, one in zip(entries, role_one, strict=True) if entry)

        @pl.when(code >= 512)
        def _():
            p = piece(lax.rem(code, 4), lax.rem(lax.div(code, 4), 2), lax.rem(lax.div(code, 8), 2))
            sub = lax.rem(lax.div(code, 16), 4)
            ref = rows.at[p, pl.ds(pl.multiple_of(sub * SUB, SUB), SUB)]
            arrived(ref, rsem.at[p, sub])
            for i, d in enumerate(DIRS):
                bit = 64 << i
                if any(entry & bit for entry in entries):

                    @pl.when(lax.rem(lax.div(code, bit), 2) == 1)
                    def _(i=i, d=d):
                        remote(ref, ref, rsend.at[i], rsem.at[p, sub], targets[d])

    def col_arrival(dx, q, sub):
        if (dx, q) != (0, 0):
            p = piece(dx, q, 0)
            arrived(col_part(p, sub), csem.at[p, sub])
            if dx == 3 and sub < 2:
                col_send(p, sub, right)
            if dx == 1 and sub >= 2:
                col_send(p, sub, left)
            col_send(p, sub, partner)
        root_take(piece(dx, q, 0), sub)

    def other_arrival(dx, q, sub):
        p = piece(dx, q, 1)
        arrived(col_part(p, sub), csem.at[p, sub])
        root_take(p, sub)

    def spread_across():
        p = piece(0, 1, 0)
        for i in range(4):
            col_send(p, i, right)
            col_send(p, (i + 2) % 4, left)

    block = hacc.shape[0] // 4

    def hessian(dx0, q0, dx1, q1, half, place):
        chips = [lax.rem(x + dx, 4) * 2 + lax.rem(zh + q, 2) for dx, q in ((dx0, q0), (dx1, q1))]

        @pl.loop(0, 2)
        def _(i):
            off = pl.multiple_of((2 * half + i) * block, block)
            sl = pl.ds(off, block)
            row_side = jnp.concatenate(
                [rows[pl.ds(2 * kk, 2), :, pl.ds(off, block)].reshape(2 * PIECE, block) for kk in chips], axis=0
            )
            col_side = jnp.concatenate([cols[pl.ds(2 * kk, 2)].reshape(2 * PIECE, feats) for kk in chips], axis=0)
            part = lax.dot_general(row_side, col_side, (((0,), (0,)), ((), ())), preferred_element_type=F32)
            if place > 0:
                hacc[sl] = part
            elif place < 0:
                out_h[sl] = ((hacc[sl] + part) * (1.0 / tokens)).astype(BF16)
            else:
                hacc[sl] += part

    def residual(i):
        if i == 0:
            s_copy.wait()
            scol[...] = sbuf[...].T
        a, b = wt_copies[i]
        a.wait()
        b.wait()
        step = 64

        @pl.loop(0, quarter // step)
        def _(j):
            sl = pl.ds(pl.multiple_of(i * quarter + j * step, step), step)
            for g in range(feats // 128):
                lanes = pl.ds(g * 128, 128)
                value = cbuf[sl, lanes].astype(F32) * scol[sl, g : g + 1]
                res[sl, lanes] = (res[sl, lanes].astype(F32) - value).astype(BF16)

    share = rank // 8

    def narrow_rows(who):
        return pl.ds(pl.multiple_of(who * share, share), share)

    def narrow_block(ref, who):
        return ref.at[narrow_rows(who)]

    def y_block(who):
        return yt.at[w, narrow_rows(who)]

    def y_piece(p):
        return yt.at[p]

    def sum_of(ref, sem):
        for j in range(1, 8):
            arrived(ref.at[peer(j)], sem.at[peer(j)])
        total = ref[0].astype(F32)
        for j in range(1, 8):
            total += ref[j].astype(F32)
        return total

    def y_dot():
        rn_copy.wait()
        ypt[...] = jnp.dot(cols[w], rn[...], preferred_element_type=F32).T
        for j in range(1, 8):
            to = peer(j)
            remote(narrow_block(ypt, to), yrecv.at[n], yrs_s.at[0], yrs_r.at[n], (w, to))
        yrecv[n] = ypt[narrow_rows(n)]

    def y_reduce():
        yt[w, narrow_rows(n)] = sum_of(yrecv, yrs_r).astype(BF16)
        for j in range(1, 8):
            remote(y_block(n), y_block(n), yag_s.at[0], yag_r.at[n], (w, peer(j)))

    def y_half(p, h):
        return yt.at[p, pl.ds(h * (rank // 2), rank // 2)]

    def y_send(p, to):
        remote(y_piece(p), y_piece(p), ywd_s.at[0], ywd_r.at[p, 0], to)

    def y_half_send(p, h, to):
        remote(y_half(p, h), y_half(p, h), ywd_s.at[0], ywd_r.at[p, h], to)

    def y_spread():
        for j in range(1, 8):
            arrived(y_block(peer(j)), yag_r.at[peer(j)])
        for to in (right, left, across, partner):
            y_send(w, to)

    def y_across():
        p = piece(0, 1, 0)
        arrived(y_piece(p), ywd_r.at[p, 0])
        for to in (right, left, partner):
            y_send(p, to)

    def y_beside(dx, q):
        p = piece(dx, q, 0)
        arrived(y_piece(p), ywd_r.at[p, 0])
        y_half_send(p, int(dx == 1), left if dx == 1 else right)
        y_send(p, partner)

    def y_opposite(q):
        p = piece(2, q, 0)
        for h in range(2):
            arrived(y_half(p, h), ywd_r.at[p, h])
        y_send(p, partner)

    def y_others():
        for dx in range(4):
            for q in range(2):
                p = piece(dx, q, 1)
                arrived(y_piece(p), ywd_r.at[p, 0])

    hblock = feats // 4

    def h_times_r(b):
        lanes = pl.ds(b * hblock, hblock)
        every = jnp.concatenate([yt[p] for p in range(16)], axis=1)
        value = jnp.dot(every, cols[:, :, lanes].reshape(tokens, hblock), preferred_element_type=F32)
        hrt[:, lanes] = (value * (1.0 / tokens)).astype(BF16)

    def product(b):
        sl = pl.ds(b * quarter, quarter)
        value = lax.dot_general(res[sl], hrt[...], (((1,), (1,)), ((), ())), preferred_element_type=F32)
        prod[sl] = value.astype(BF16)

    own_rows = out_rows // 8

    def prod_rows(who):
        return pl.ds(pl.multiple_of(who * own_rows, own_rows), own_rows)

    def product_send(j):
        to = peer(j)
        remote(prod.at[prod_rows(to)], prodrecv.at[n], prs_s.at[0], prs_r.at[n], (w, to))
        if j == 1:
            prodrecv[n] = prod[prod_rows(n)]

    gshare = rank // 16

    def gram_rows(ref, who):
        return ref.at[pl.ds(pl.multiple_of(who * gshare, gshare), gshare)]

    def gram_part():
        gpart[...] = jnp.dot(hrt[...], rn[...], preferred_element_type=F32)
        for j in range(1, 8):
            to = peer(j)
            remote(gram_rows(gpart, w), grecv.at[n], grs_s.at[0], grs_r.at[n], (w, to))
        grecv[n] = gpart[pl.ds(pl.multiple_of(w * gshare, gshare), gshare)]

    def gram_send(p, to):
        remote(gram_rows(gall, p), gram_rows(gall, p), gag_s.at[0], gag_r.at[p], to)

    def gram_reduce():
        gall[pl.ds(pl.multiple_of(w * gshare, gshare), gshare)] = sum_of(grecv, grs_r)
        for j in range(1, 8):
            gram_send(w, (lax.rem(k + j, 8) * 2 + c, n))
        gram_send(w, partner)

    steps = {
        "c": col_arrival, "o": other_arrival, "Q": spread_across, "H": hessian, "res": residual,
        "ydot": y_dot, "yred": y_reduce, "yag": y_spread, "ya": y_across, "yn": y_beside, "yf": y_opposite, "yoth": y_others,
        "hr": h_times_r, "prod": product, "prodsend": product_send, "gram": gram_part, "gramred": gram_reduce,
    }
    for name, *rest in PLAN:
        if name == "r":
            row_step(rest)
        else:
            steps[name](*rest)

    for j in range(1, 8):
        p = lax.rem(k + j, 8) * 2 + c
        arrived(gram_rows(gall, p), gag_r.at[p])
        gram_send(p, partner)
    out_prod[...] = sum_of(prodrecv, prs_r)
    for j in range(8):
        p = lax.rem(k + j, 8) * 2 + 1 - c
        arrived(gram_rows(gall, p), gag_r.at[p])
    out_gram[...] = gall[...].T

    arrived(hacc.at[pl.ds(0, len(col_sends) * 16)], csend.at[0])
    for r in range(8):

        @pl.when(is_role[r])
        def _(r=r):
            for i in range(3):
                sent = sum(1 for step in PLAN if step[0] == "r" and step[1 + r] & (64 << i))
                if sent:
                    arrived(hacc.at[pl.ds(0, sent * 8)], rsend.at[i])

    arrived(yrecv.at[pl.ds(0, 7)], yrs_s.at[0])
    arrived(ypt.at[pl.ds(0, 7 * share // 2)], yag_s.at[0])
    arrived(yt.at[pl.ds(0, 15)], ywd_s.at[0])
    arrived(prodrecv.at[pl.ds(0, 7)], prs_s.at[0])
    arrived(grecv.at[pl.ds(0, 7)], grs_s.at[0])
    arrived(gpart.at[pl.ds(0, 15 * gshare)], gag_s.at[0])


def store(prod, gram, hess, out_prod, out_gram, out_h, sem):
    copies = [
        pltpu.make_async_copy(src, dst, sem.at[i])
        for i, (src, dst) in enumerate(((hess, out_h), (prod, out_prod), (gram, out_gram)))
    ]
    for copy in copies:
        copy.start()
    for copy in copies:
        copy.wait()


def body(activations, weight_tile, codes, group_scales, right_factor):
    piece_tokens, feats = activations.shape
    out_rows = weight_tile.shape[0]
    rank = right_factor.shape[1]
    groups = group_scales.shape[1]
    assert piece_tokens == PIECE
    dma = pltpu.SemaphoreType.DMA
    any_spec = pl.BlockSpec(memory_space=pl.ANY)
    vmem_spec = pl.BlockSpec(memory_space=pltpu.VMEM)
    shapes = (((out_rows // 8, rank), F32), ((rank, rank), F32), ((out_rows, feats), BF16))
    parts = pl.pallas_call(
        kernel,
        out_shape=tuple(pltpu.VMEM(s, d) for s, d in shapes),
        in_specs=[any_spec] * 5,
        out_specs=(vmem_spec,) * 3,
        scratch_shapes=[
            pltpu.VMEM((16, PIECE, feats), BF16),
            pltpu.VMEM((16, PIECE, feats // 2), BF16),
            pltpu.VMEM((out_rows, feats), F32),
            pltpu.VMEM((out_rows, feats), BF16),
            pltpu.VMEM((out_rows, feats), jnp.int32),
            pltpu.VMEM((groups, out_rows), F32),
            pltpu.VMEM((out_rows, groups), F32),
            pltpu.VMEM((feats, rank), BF16),
            pltpu.VMEM((rank, PIECE), F32),
            pltpu.VMEM((8, rank // 8, PIECE), F32),
            pltpu.VMEM((16, rank, PIECE), BF16),
            pltpu.VMEM((rank, feats), BF16),
            pltpu.VMEM((out_rows, rank), BF16),
            pltpu.VMEM((8, out_rows // 8, rank), BF16),
            pltpu.VMEM((rank, rank), F32),
            pltpu.VMEM((8, rank // 16, rank), F32),
            pltpu.VMEM((rank, rank), F32),
            dma((11,)),
            dma((16, 4)),
            dma((1,)),
            dma((16, 4)),
            dma((3,)),
            dma((8,)), dma((1,)), dma((8,)), dma((1,)), dma((16, 2)), dma((1,)),
            dma((8,)), dma((1,)), dma((8,)), dma((1,)), dma((16,)), dma((1,)),
        ],
        compiler_params=pltpu.CompilerParams(
            collective_id=0, has_side_effects=True, vmem_limit_bytes=52 << 20
        ),
    )(activations, weight_tile, codes, group_scales.T, right_factor)
    return tuple(pl.pallas_call(
        store,
        out_shape=tuple(jax.ShapeDtypeStruct(s, d) for s, d in shapes),
        in_specs=[vmem_spec] * 3,
        out_specs=(any_spec,) * 3,
        scratch_shapes=[dma((3,))],
        compiler_params=pltpu.CompilerParams(vmem_limit_bytes=8 << 20),
    )(*parts))


def solution(mesh):
    spec = P("wide", "narrow")
    return jax.shard_map(
        body,
        mesh=mesh,
        in_specs=(spec, spec, spec, spec, P()),
        out_specs=(P(("wide", "narrow"), None), P(), spec),
        check_vma=False,
    )
```

time: 525 us -> 91.5 us (0.17)
  the two profiles are of different devices: /device:TPU:0 before, /device:TPU:97 now
where the time goes in v2:
time: 91.5 us; the launch traced here: 91.4 us
  Pallas kernels  90.6 us (99%)
    pallas_call x1, Pallas kernels, body(): pl.pallas_call(kernel, out_shape=tuple((pltpu.VMEM(s, d) for s, d in shap...  88.4 us
    pallas_call x1, Pallas kernels, body(): pl.pallas_call(store, out_shape=tuple((jax.ShapeDtypeStruct(s, d) for s,...  2.15 us

profile of v2, /device:TPU:97, one launch (start us, length us, event | category | flops | bytes accessed | tf_op | source)
XLA Modules:
  0.0 91.4 jit_solution(4300884225096091687)
XLA Ops:
  0.6 88.4 %shard_map.76 = (f32[128,256]{1,0:T(8,128)S(1)}, f32[256,256]{1,0:T(8,128)S(1)}, bf16[1024,2048]{1,0:T(8,128)(2,1)S(1)}) custom-call(bf16[128,2048]{1,0:T(8,128)(2,1)} %act.1, bf16[1024,2048]{1,0:T(8,128)(2,1)} %wt.1, s32[1024,2048]{1,0:T(8,128)} %codes.1, f32[16,1024]{1,0:T(8,128)} %bitcast.1, bf16[16384,256]{1,0:T(8,128)(2,1)} %rf.1), custom_call_target="tpu_custom_call" | custom-call | tf_op jit(solution)/shard_map/pallas_call | solution.py:625
  89.1 2.1 %shard_map.77 = (f32[128,256]{1,0:T(8,128)}, f32[256,256]{1,0:T(8,128)}, bf16[1024,2048]{1,0:T(8,128)(2,1)}) custom-call(f32[128,256]{1,0:T(8,128)S(1)} %get-tuple-element.6.prod, f32[256,256]{1,0:T(8,128)S(1)} %get-tuple-element.7.gram, bf16[1024,2048]{1,0:T(8,128)(2,1)S(1)} %get-tuple-element.8.hess), custom_call_target="tpu_custom_call" | custom-call | tf_op jit(solution)/shard_map/pallas_call | solution.py:660

commit v3 on v2

--- a/solution.py
+++ b/solution.py
@@ -215,7 +215,6 @@
     ("r", 0, 549, 513, 538, 522, 799, 794, 927),
     ("r", 0, 541, 886, 0, 0, 655, 703, 0),
     ("r", 0, 575, 910, 0, 0, 0, 0, 0),
-    ("prod", 1),
     ("r", 0, 0, 554, 525, 615, 695, 669, 789),
     ("r", 0, 0, 0, 0, 685, 853, 589, 0),
     ("prod", 0),
@@ -223,11 +222,10 @@
     ("r", 0, 543, 0, 518, 517, 0, 805, 623),
     ("r", 0, 0, 0, 0, 0, 0, 0, 637),
     ("r", 0, 0, 0, 0, 0, 0, 0, 806),
-    ("prod", 2),
     ("r", 0, 0, 538, 543, 0, 870, 799, 0),
     ("r", 0, 0, 0, 0, 0, 514, 630, 0),
     ("r", 0, 0, 0, 0, 0, 669, 0, 0),
-    ("prod", 3),
+    ("prod", 1),
     ("r", 0, 533, 0, 566, 527, 0, 582, 942),
     ("r", 0, 526, 0, 533, 559, 0, 0, 589),
     ("gram",),
@@ -526,7 +524,7 @@
         hrt[:, lanes] = (value * (1.0 / tokens)).astype(BF16)
 
     def product(b):
-        sl = pl.ds(b * quarter, quarter)
+        sl = pl.ds(b * (out_rows // 2), out_rows // 2)
         value = lax.dot_general(res[sl], hrt[...], (((1,), (1,)), ((), ())), preferred_element_type=F32)
         prod[sl] = value.astype(BF16)
 
@@ -602,10 +600,14 @@
 
 
 def store(prod, gram, hess, out_prod, out_gram, out_h, sem):
+    parts = 8
+    step = hess.shape[0] // parts
     copies = [
-        pltpu.make_async_copy(src, dst, sem.at[i])
-        for i, (src, dst) in enumerate(((hess, out_h), (prod, out_prod), (gram, out_gram)))
+        pltpu.make_async_copy(hess.at[pl.ds(i * step, step)], out_h.at[pl.ds(i * step, step)], sem.at[i])
+        for i in range(parts)
     ]
+    copies.append(pltpu.make_async_copy(prod, out_prod, sem.at[parts]))
+    copies.append(pltpu.make_async_copy(gram, out_gram, sem.at[parts + 1]))
     for copy in copies:
         copy.start()
     for copy in copies:
@@ -662,7 +664,7 @@
         out_shape=tuple(jax.ShapeDtypeStruct(s, d) for s, d in shapes),
         in_specs=[vmem_spec] * 3,
         out_specs=(any_spec,) * 3,
-        scratch_shapes=[dma((3,))],
+        scratch_shapes=[dma((10,))],
         compiler_params=pltpu.CompilerParams(vmem_limit_bytes=8 << 20),
     )(*parts))
 

time: 91.5 us -> 91.3 us (level)
  the two profiles are of different devices: /device:TPU:97 before, /device:TPU:0 now
where the time goes in v3:
time: 91.3 us; the launch traced here: 89.8 us
  Pallas kernels  89 us (97%)
    pallas_call x1, Pallas kernels, body(): pl.pallas_call(kernel, out_shape=tuple((pltpu.VMEM(s, d) for s, d in shap...  86.8 us
    pallas_call x1, Pallas kernels, body(): pl.pallas_call(store, out_shape=tuple((jax.ShapeDtypeStruct(s, d) for s,...  2.21 us

profile of v3, /device:TPU:0, one launch (start us, length us, event | category | flops | bytes accessed | tf_op | source)
XLA Modules:
  0.0 89.8 jit_solution(14300082842882195941)
XLA Ops:
  0.6 86.8 %shard_map.76 = (f32[128,256]{1,0:T(8,128)S(1)}, f32[256,256]{1,0:T(8,128)S(1)}, bf16[1024,2048]{1,0:T(8,128)(2,1)S(1)}) custom-call(bf16[128,2048]{1,0:T(8,128)(2,1)} %act.1, bf16[1024,2048]{1,0:T(8,128)(2,1)} %wt.1, s32[1024,2048]{1,0:T(8,128)} %codes.1, f32[16,1024]{1,0:T(8,128)} %bitcast.1, bf16[16384,256]{1,0:T(8,128)(2,1)} %rf.1), custom_call_target="tpu_custom_call" | custom-call | tf_op jit(solution)/shard_map/pallas_call | solution.py:627
  87.5 2.2 %shard_map.77 = (f32[128,256]{1,0:T(8,128)}, f32[256,256]{1,0:T(8,128)}, bf16[1024,2048]{1,0:T(8,128)(2,1)}) custom-call(f32[128,256]{1,0:T(8,128)S(1)} %get-tuple-element.6.prod, f32[256,256]{1,0:T(8,128)S(1)} %get-tuple-element.7.gram, bf16[1024,2048]{1,0:T(8,128)(2,1)S(1)} %get-tuple-element.8.hess), custom_call_target="tpu_custom_call" | custom-call | tf_op jit(solution)/shard_map/pallas_call | solution.py:662
